TPU v7x, 32 devices: a whole 2x2x4 slice. The times are simulated.
32 devices in a mesh: req: 16 (over z, y, core), grp: 2 (over x).
Axes of the slice: x: 2, y: 2, z: 4, core: 2. Of those that a mesh axis runs over, the one named last changes fastest.
Arguments:
- tokens: bfloat16 [8192, 1024], P('req'), may hold values from -6 to 6
- norm_attn: float32 [1024], replicated, may hold values from 0.25 to 1.75
- w_query: bfloat16 [1024, 1024], P(None, 'grp'), may hold values from -0.1875 to 0.1875
- w_key: bfloat16 [1024, 1024], P(None, 'grp'), may hold values from -0.1875 to 0.1875
- w_value: bfloat16 [1024, 1024], P(None, 'grp'), may hold values from -0.1875 to 0.1875
- w_out: bfloat16 [1024, 1024], P('grp'), may hold values from -0.1875 to 0.1875
- persist_keys: bfloat16 [16, 1024], P(None, 'grp'), may hold values from -5 to 5
- persist_values: bfloat16 [16, 1024], P(None, 'grp'), may hold values from -5 to 5
- kv_cache: bfloat16 [768, 2, 128, 1024], P('req', None, None, 'grp'), may hold values from -160 to 160
- slot_request: int32 [768], P('req'), may hold values from 0 to 255, as said below
- slot_page: int32 [768], P('req'), may hold values from 0 to 48, as said below
- cache_len: int32 [256], P('req'), may hold values from 1 to 2304
- tree_mask: int32 [256, 32, 32], P('req'), may hold values from 0 to 1, as said below
- accept_path: int32 [256, 8], P('req'), may hold values from 0 to 31, as said below
- accept_len: int32 [256], P('req'), may hold values from 1 to 8
- memory: float32 [256, 8, 128, 128], P('req', 'grp'), may hold values from -4 to 4
- momentum: float32 [256, 8, 128, 128], P('req', 'grp'), may hold values from -1.2 to 1.2
- momentum_code: int32 [256, 8, 8], P('req', None, 'grp'), may hold values from 0 to 15
- forget_code: int32 [256, 8, 8], P('req', None, 'grp'), may hold values from 0 to 15
- norm_ffn: float32 [1024], replicated, may hold values from 0.25 to 1.75
- w_gate_up: bfloat16 [2, 1024, 2816], P(None, None, 'grp'), may hold values from -0.1875 to 0.1875
- w_down: bfloat16 [2816, 1024], P('grp'), may hold values from -0.109375 to 0.109375
Outputs:
- layer_out: bfloat16 [8192, 1024], P(('req', 'grp'))
- memory_out: float32 [256, 8, 128, 128], P('req', 'grp')
- momentum_out: float32 [256, 8, 128, 128], P('req', 'grp')
Inputs may be any that keep to these rules, and one draw needn't show every extreme that they name: `slot_request`: slot s lies with index s // 48 of req; slots s with (s % 48) // 3 = j hold pages of requests j * 16 to (j + 1) * 16 - 1 only. The live pages 0 .. ceil(cache_len[r] / 128) - 1 of every request stand each in exactly one slot; every other slot has page number 16 * 3. `slot_page`: see slot_request. `tree_mask`: each node's parent precedes it; node 0 is the root; rows include the node itself. `accept_path`: entry n is the node at depth n on the root path of one draft node.
All inputs are finite; a program needn't handle non-finite values.
Results may differ from a plain program's by a relative error of at most 0.015.
Values may be sent and summed in bfloat16 or wider, within the bound.
No kernel may reach another device: no remote copies, remote signals or barrier semaphores. Data moves between devices by JAX's collectives and lax.ppermute only.
A program may use at most 192 MiB of HBM per device.

v0:
```python
import math
import jax
import jax.numpy as jnp
from jax import lax
from jax.sharding import PartitionSpec as P

HD = 128
EPS = 1e-06
THETA = 0.5
NEG = -1e30


def rms_norm(rows, gain):
    values = rows.astype(jnp.float32)
    factor = lax.rsqrt(jnp.mean(values * values, axis=-1, keepdims=True) + EPS)
    return (values * factor * gain).astype(jnp.bfloat16)


def unit_rows(vectors):
    return vectors * lax.rsqrt(jnp.sum(vectors * vectors, axis=-1, keepdims=True) + EPS)


def page_partials(pages, page_queries, page_first, page_limit, scale):
    count = pages.shape[0]
    page_len = pages.shape[2]
    width = pages.shape[3]
    heads = width // HD
    draft = page_queries.shape[1]
    query_four = page_queries.reshape(count, draft, heads, HD)
    key_four = pages[:, 0].reshape(count, page_len, heads, HD)
    value_four = pages[:, 1].reshape(count, page_len, heads, HD)
    scores = (
        jnp.einsum("sihd,sthd->shit", query_four, key_four, preferred_element_type=jnp.float32)
        * scale
    )
    position = page_first[:, None] + jnp.arange(page_len, dtype=jnp.int32)[None, :]
    valid = (position < page_limit[:, None])[:, None, None, :]
    masked = jnp.where(valid, scores, NEG)
    top = jnp.max(masked, axis=3)
    weight = jnp.where(valid, jnp.exp(masked - top[..., None]), 0.0)
    total = jnp.sum(weight, axis=3)
    numer = jnp.einsum(
        "shit,sthd->sihd",
        weight.astype(jnp.bfloat16),
        value_four,
        preferred_element_type=jnp.float32,
    )
    return (numer.reshape(count, draft, width), top, total)


def on_device(
    tokens,
    norm_attn,
    w_query,
    w_key,
    w_value,
    w_out,
    persist_keys,
    persist_values,
    kv_cache,
    slot_request,
    slot_page,
    cache_len,
    tree_mask,
    accept_path,
    accept_len,
    memory,
    momentum,
    momentum_code,
    forget_code,
    norm_ffn,
    w_gate_up,
    w_down,
):
    group_rows = tokens.shape[0]
    reqs = cache_len.shape[0]
    draft = tree_mask.shape[1]
    width = w_query.shape[1]
    heads = width // HD
    fixed_count = persist_keys.shape[0]
    page_len = kv_cache.shape[2]
    scale = 1.0 / math.sqrt(HD)
    normed = rms_norm(tokens, norm_attn)
    queries = jnp.dot(normed, w_query, preferred_element_type=jnp.float32).astype(jnp.bfloat16)
    keys = jnp.dot(normed, w_key, preferred_element_type=jnp.float32).astype(jnp.bfloat16)
    values = jnp.dot(normed, w_value, preferred_element_type=jnp.float32).astype(jnp.bfloat16)
    query_four = queries.reshape(reqs, draft, heads, HD)
    key_four = keys.reshape(reqs, draft, heads, HD)
    value_four = values.reshape(reqs, draft, heads, HD)
    fixed_keys = persist_keys.reshape(fixed_count, heads, HD)
    fixed_values = persist_values.reshape(fixed_count, heads, HD)
    tree_scores = (
        jnp.einsum("rihd,rjhd->rhij", query_four, key_four, preferred_element_type=jnp.float32)
        * scale
    )
    tree_scores = jnp.where(tree_mask[:, None] == 1, tree_scores, NEG)
    fixed_scores = (
        jnp.einsum("rihd,phd->rhip", query_four, fixed_keys, preferred_element_type=jnp.float32)
        * scale
    )
    local_scores = jnp.concatenate([fixed_scores, tree_scores], axis=3)
    local_top = jnp.max(local_scores, axis=3)
    local_weight = jnp.exp(local_scores - local_top[..., None])
    local_total = jnp.sum(local_weight, axis=3)
    local_rounded = local_weight.astype(jnp.bfloat16)
    local_numer = jnp.einsum(
        "rhip,phd->rihd",
        local_rounded[..., :fixed_count],
        fixed_values,
        preferred_element_type=jnp.float32,
    )
    local_numer = local_numer + jnp.einsum(
        "rhij,rjhd->rihd",
        local_rounded[..., fixed_count:],
        value_four,
        preferred_element_type=jnp.float32,
    )
    first_request = lax.axis_index("req") * reqs
    request_ids = jnp.arange(reqs, dtype=jnp.int32)
    moved_pages, moved_request, moved_page = (
        lax.all_to_all(kv_cache, "req", split_axis=0, concat_axis=0, tiled=True),
        lax.all_to_all(slot_request, "req", split_axis=0, concat_axis=0, tiled=True),
        lax.all_to_all(slot_page, "req", split_axis=0, concat_axis=0, tiled=True),
    )
    local_request = moved_request - first_request
    pick = local_request[:, None] == request_ids[None, :]
    limits = jnp.sum(jnp.where(pick, cache_len[None, :], 0), axis=1)
    page_queries = queries.reshape(reqs, draft, width)[local_request]
    numer, top, total = page_partials(
        moved_pages, page_queries, moved_page * page_len, limits, scale
    )
    slot_count = numer.shape[0]
    pick_weight = pick.astype(jnp.float32)
    request_top = jnp.max(jnp.where(pick[:, :, None, None], top[:, None], NEG), axis=0)
    best = jnp.maximum(request_top, local_top)
    slot_best = jnp.einsum("sr,rhi->shi", pick_weight, best, precision=lax.Precision.HIGHEST)
    factor = jnp.exp(top - slot_best)
    scaled = (
        numer.reshape(slot_count, draft, heads, HD) * jnp.transpose(factor, (0, 2, 1))[..., None]
    )
    page_numer = jnp.einsum("sr,sihd->rihd", pick_weight, scaled, precision=lax.Precision.HIGHEST)
    page_total = jnp.einsum(
        "sr,shi->rhi", pick_weight, total * factor, precision=lax.Precision.HIGHEST
    )
    local_factor = jnp.exp(local_top - best)
    numer_all = local_numer * jnp.transpose(local_factor, (0, 2, 1))[..., None] + page_numer
    total_all = local_total * local_factor + page_total
    attention = numer_all / jnp.transpose(total_all, (0, 2, 1))[..., None]
    unit_query = unit_rows(query_four.astype(jnp.float32))
    retrieved = jnp.einsum("rihd,rhde->rihe", unit_query, memory, precision=lax.Precision.HIGHEST)
    mixed = (attention + retrieved).reshape(group_rows, width).astype(jnp.bfloat16)
    rows = group_rows // lax.axis_size("grp")
    head_sum = lax.psum_scatter(
        jnp.dot(mixed, w_out, preferred_element_type=jnp.float32).astype(jnp.bfloat16),
        "grp",
        scatter_dimension=0,
        tiled=True,
    ).astype(jnp.float32)
    own_rows = lax.dynamic_slice_in_dim(tokens, lax.axis_index("grp") * rows, rows, 0)
    residual = (own_rows.astype(jnp.float32) + head_sum).astype(jnp.bfloat16)
    ffn_in = rms_norm(residual, norm_ffn)
    piece = lax.all_gather(ffn_in, "grp", axis=0, tiled=True)
    gate = jnp.dot(piece, w_gate_up[0], preferred_element_type=jnp.float32)
    up = jnp.dot(piece, w_gate_up[1], preferred_element_type=jnp.float32)
    hidden = (jax.nn.silu(gate) * up).astype(jnp.bfloat16)
    ffn_out = lax.psum_scatter(
        jnp.dot(hidden, w_down, preferred_element_type=jnp.float32).astype(jnp.bfloat16),
        "grp",
        scatter_dimension=0,
        tiled=True,
    ).astype(jnp.float32)
    layer_out = (residual.astype(jnp.float32) + ffn_out).astype(jnp.bfloat16)
    req_rows = request_ids[:, None]
    path_keys = unit_rows(key_four[req_rows, accept_path].astype(jnp.float32))
    path_values = value_four[req_rows, accept_path].astype(jnp.float32)
    eta = 0.97 - 0.06 * momentum_code.astype(jnp.float32)
    forget = 0.01 + 0.02 * forget_code.astype(jnp.float32)
    for step in range(accept_path.shape[1]):
        unit = path_keys[:, step]
        predicted = jnp.einsum("rhd,rhde->rhe", unit, memory, precision=lax.Precision.HIGHEST)
        grad = jnp.einsum(
            "rhd,rhe->rhde", unit, predicted - path_values[:, step], precision=lax.Precision.HIGHEST
        )
        new_mom = eta[:, step, :, None, None] * momentum - THETA * grad
        new_mem = (1.0 - forget[:, step, :, None, None]) * memory + new_mom
        live = (step < accept_len)[:, None, None, None]
        momentum = jnp.where(live, new_mom, momentum)
        memory = jnp.where(live, new_mem, memory)
    return (layer_out, memory, momentum)


def solution(mesh):
    return jax.shard_map(
        on_device,
        mesh=mesh,
        in_specs=(
            P("req", None),
            P(),
            P(None, "grp"),
            P(None, "grp"),
            P(None, "grp"),
            P("grp", None),
            P(None, "grp"),
            P(None, "grp"),
            P("req", None, None, "grp"),
            P("req"),
            P("req"),
            P("req"),
            P("req", None, None),
            P("req", None),
            P("req"),
            P("req", "grp", None, None),
            P("req", "grp", None, None),
            P("req", None, "grp"),
            P("req", None, "grp"),
            P(),
            P(None, None, "grp"),
            P("grp", None),
        ),
        out_specs=(
            P(("req", "grp"), None),
            P("req", "grp", None, None),
            P("req", "grp", None, None),
        ),
        check_vma=False,
    )
```

profile of v0, /device:TPU:0, one launch (start us, length us, event | category | flops | bytes accessed | tf_op | source)
XLA Modules:
  0.0 470.7 jit_solution(17253716148561162837)
XLA Ops:
  8.7 7.4 %all-to-all-start = ((s32[16,3,1]{1,2,0:T(1,128)}), s32[16,3,1]{1,2,0:T(1,128)S(1)}, u32[]{:S(2)}, u32[]{:S(2)}) async-start(s32[16,3,1]{1,2,0:T(1,128)} %bitcast.6), calls=%async_computation | async-start | bytes 16384 | tf_op jit(solution)/shard_map/all_to_all | solution.py:122
  17.4 5.0 %all-to-all-done = s32[16,3,1]{1,2,0:T(1,128)S(1)} async-done(((s32[16,3,1]{1,2,0:T(1,128)}), s32[16,3,1]{1,2,0:T(1,128)S(1)}, u32[]{:S(2)}, u32[]{:S(2)}) %all-to-all-start) | async-done | bytes 224 | tf_op jit(solution)/shard_map/all_to_all | solution.py:122
  22.4 3.5 all-to-all-start.1
  25.9 16.7 %copy.234 = bf16[48,2,128,512]{2,3,1,0:T(8,128)(2,1)} copy(bf16[48,2,128,512]{3,2,1,0:T(8,128)(2,1)} %param.30) | data formatting | bytes 25165824 | tf_op args[8]
  43.2 6.0 %all-to-all-start.2 = ((bf16[48,2,128,512]{2,3,1,0:T(8,128)(2,1)}), bf16[48,2,128,512]{2,3,1,0:T(8,128)(2,1)}, u32[]{:S(2)}, u32[]{:S(2)}) async-start(bf16[48,2,128,512]{2,3,1,0:T(8,128)(2,1)} %copy.234), calls=%async_computation.2 | async-start | bytes 25165824 | tf_op jit(solution)/shard_map/all_to_all | solution.py:121
  51.4 3.1 convolution_convert_fusion.4
  55.7 3.1 convolution_convert_fusion.3
  58.8 2.0 reshape.250
  60.7 2.2 fusion.143
  62.9 2.4 copy.225
  65.3 3.1 convolution_convert_fusion.2
  68.4 2.0 reshape.252
  70.5 2.0 gather_fusion.1
  72.5 2.6 gather_fusion.2
  94.5 5.5 %fusion.145 = f32[16,4,1,128]{3,2,1,0:T(1,128)S(1)} fusion(f32[16,4,128,1]{2,3,1,0:T(1,128)S(1)} %bitcast.263, f32[16,4,128,128]{3,2,1,0:T(8,128)} %param.37), kind=kOutput, calls=%fused_computation.235 | convolution fusion | flops 12582912 | bytes 4259840 | tf_op jit(solution)/shard_map/rhd,rhde->rhe/dot_general | solution.py:180
  100.0 6.6 %fusion.36 = f32[16,4,1,128]{3,2,1,0:T(1,128)S(1)} fusion(f32[16,4,128,1]{2,3,1,0:T(1,128)S(1)} %bitcast.262, f32[16,4,128,128]{3,2,1,0:T(8,128)} %param.37, f32[16,4,128,128]{3,2,1,0:T(8,128)S(1)} %copy-done.1, f32[16,4,128]{2,1,0:T(4,128)S(1)} %fusion.104, f32[16,4,128]{2,1,0:T(4,128)S(1)} %get-tuple-element.14, f32[16,4]{1,0:T(8,128)S(1)} %copy.260, ...), kind=kOutput, calls=%fused_computation.61 | convolution fusion | flops 19922944 | bytes 8520208 | tf_op jit(solution)/shard_map/rhd,rhde->rhe/dot_general | solution.py:180
  106.7 3.6 add_select_fusion.6
  110.3 3.7 fusion.146
  114.0 7.9 %fusion.30 = f32[16,4,1,128]{3,2,1,0:T(1,128)S(1)} fusion(f32[16,4,128,1]{2,3,1,0:T(1,128)S(1)} %bitcast.272, f32[16,4,128,128]{3,2,1,0:T(8,128)S(1)} %add_select_fusion.6, f32[16,4,128]{2,1,0:T(4,128)S(1)} %fusion.102, f32[16,4,128]{2,1,0:T(4,128)S(1)} %get-tuple-element.16, f32[16,4]{1,0:T(8,128)S(1)} %copy-done.30, f32[16,4]{1,0:T(8,128)S(1)} %copy-done.50, ...), kind=kOutput, calls=%fused_computation.55 | convolution fusion | flops 30408704 | bytes 8651824 | tf_op jit(solution)/shard_map/rhd,rhde->rhe/dot_general | solution.py:180
  122.0 6.4 %add_select_fusion.4 = f32[16,4,128,128]{3,2,1,0:T(8,128)S(1)} fusion(f32[16,4,128]{2,1,0:T(4,128)S(1)} %fusion.101, f32[16,4,128]{2,1,0:T(4,128)S(1)} %get-tuple-element.17, f32[16,4]{1,0:T(8,128)S(1)} %copy-done.32, f32[16,4,128]{2,1,0:T(4,128)S(1)} %fusion.102, f32[16,4,128,128]{3,2,1,0:T(8,128)S(1)} %add_select_fusion.6, ...), kind=kLoop, calls=%fused_computation.17 | loop fusion | flops 26214400 | bytes 12846656 | tf_op jit(solution)/shard_map/jit(_where)/select_n | solution.py:188
  128.4 3.6 fusion.147
  132.2 2.0 fusion.144
  134.2 5.7 %fusion.6 = f32[16,4,128,128]{3,2,1,0:T(8,128)S(1)} fusion(f32[16,4,128]{2,1,0:T(4,128)S(1)} %fusion.101, f32[16,4,128]{2,1,0:T(4,128)S(1)} %get-tuple-element.17, f32[16,4]{1,0:T(8,128)S(1)} %copy-done.32, f32[16,4,128]{2,1,0:T(4,128)S(1)} %fusion.102, f32[16,4,128]{2,1,0:T(4,128)S(1)} %get-tuple-element.16, f32[16,4]{1,0:T(8,128)S(1)} %copy-done.30, ...), kind=kLoop, calls=%fused_computation.19 | loop fusion | flops 20971520 | bytes 8651840 | tf_op jit(solution)/shard_map/jit(_where)/select_n | solution.py:187
  140.0 2.0 copy-done.7
  142.0 4.9 %fusion.27 = f32[16,4,1,128]{3,2,1,0:T(1,128)} fusion(f32[16,4,128,1]{2,3,1,0:T(1,128)S(1)} %bitcast.259, f32[16,4,128,128]{3,2,1,0:T(8,128)S(1)} %add_select_fusion.4, f32[16,4,128,128]{3,2,1,0:T(8,128)S(1)} %fusion.6, f32[16,4,128]{2,1,0:T(4,128)S(1)} %fusion.100, f32[16,4,128]{2,1,0:T(4,128)S(1)} %get-tuple-element.18, f32[16,4]{1,0:T(8,128)S(1)} %copy-done.36, ...), kind=kOutput, calls=%fused_computation.52 | convolution fusion | flops 19922944 | bytes 8520208 | tf_op jit(solution)/shard_map/rhd,rhde->rhe/dot_general | solution.py:180
  147.4 2.5 fusion.141
  155.9 3.0 gather_fusion
  161.5 111.4 %all-to-all-done.2 = bf16[48,2,128,512]{2,3,1,0:T(8,128)(2,1)} async-done(((bf16[48,2,128,512]{2,3,1,0:T(8,128)(2,1)}), bf16[48,2,128,512]{2,3,1,0:T(8,128)(2,1)}, u32[]{:S(2)}, u32[]{:S(2)}) %all-to-all-start.2) | async-done | bytes 12582944 | tf_op jit(solution)/shard_map/all_to_all | solution.py:121
  272.9 8.6 %fusion.142 = (bf16[48,1,128,512]{2,3,1,0:T(8,128)(2,1)}, bf16[48,1,128,512]{2,3,1,0:T(8,128)(2,1)S(1)}) fusion(bf16[48,2,128,512]{2,3,1,0:T(8,128)(2,1)} %all-to-all-done.2), kind=kLoop, calls=%fused_computation.232 | loop fusion | bytes 25165824 | tf_op jit(solution)/shard_map/slice | solution.py:31
  281.6 4.1 fusion.18
  290.4 1.7 fusion.74
  293.7 4.6 fusion.19
  298.3 5.9 %bitcast_multiply_fusion = f32[48,32,4,128]{3,1,2,0:T(8,128)S(1)} fusion(bf16[48,128,4,128]{1,3,2,0:T(8,128)(2,1)} %bitcast.250, f32[48,4,32,128]{3,2,1,0:T(8,128)S(1)} %copy-done.6, f32[48,32,4]{1,2,0:T(4,128)} %copy.244, f32[48,4,32]{2,1,0:T(4,128)} %get-tuple-element.53, pred[48,128]{1,0:T(8,128)(4,1)} %add_compare_fusion), kind=kOutput, calls=%fused_computation.30 | convolution fusion | flops 206045184 | bytes 12638208 | tf_op jit(solution)/shard_map/shit,sthd->sihd/dot_general | solution.py:42
  304.3 4.7 fusion.10
  310.6 2.6 fusion.93
  316.3 3.9 fusion.70
  320.9 1.7 convolution_convert_fusion.1
  325.9 10.3 %add_select_fusion.2 = f32[16,4,128,128]{3,2,1,0:T(8,128)S(1)} fusion(f32[16,4,128]{2,1,0:T(4,128)S(1)} %fusion.99, f32[16,4,128]{2,1,0:T(4,128)S(1)} %copy-done.26, f32[16,4]{1,0:T(8,128)S(1)} %copy.271, f32[16,4,128]{2,1,0:T(4,128)S(1)} %copy-done.22, f32[16,4,128,128]{3,2,1,0:T(8,128)} %copy-done.4, f32[16,4,128]{2,1,0:T(4,128)S(1)} %copy-done.20, ...), kind=kLoop, calls=%fused_computation.11 | loop fusion | flops 36700160 | bytes 12978272 | tf_op jit(solution)/shard_map/jit(_where)/select_n | solution.py:188
  336.3 2.0 copy-done.5
  338.3 3.7 fusion.148
  343.3 48.5 %reduce-scatter.3.cloned.1.call-done = bf16[256,1024]{1,0:T(8,128)(2,1)} async-done(((bf16[512,1024]{1,0:T(8,128)(2,1)}), bf16[256,1024]{1,0:T(8,128)(2,1)}) %reduce-scatter.3.cloned.1.call-update) | async-done | bytes 524304 | tf_op jit(solution)/shard_map/reduce_scatter | solution.py:153
  395.0 9.2 %fusion.24 = f32[16,4,1,128]{3,2,1,0:T(1,128)S(1)} fusion(f32[16,4,128,1]{2,3,1,0:T(1,128)} %bitcast.271, f32[16,4,128,128]{3,2,1,0:T(8,128)} %copy-done.5, f32[16,4,128]{2,1,0:T(4,128)} %fusion.98, f32[16,4,128]{2,1,0:T(4,128)} %get-tuple-element.20, f32[16,4]{1,0:T(8,128)} %copy.273, f32[16,4]{1,0:T(8,128)} %copy.253, ...), kind=kOutput, calls=%fused_computation.49 | convolution fusion | flops 30408704 | bytes 8651824 | tf_op jit(solution)/shard_map/rhd,rhde->rhe/dot_general | solution.py:180
  405.6 11.0 %all-gather.2.cloned.1.call-done = bf16[512,1024]{1,0:T(8,128)(2,1)} async-done(((bf16[256,1024]{1,0:T(8,128)(2,1)}), bf16[512,1024]{1,0:T(8,128)(2,1)}) %all-gather.2.cloned.1.call-update) | async-done | bytes 1048592 | tf_op jit(solution)/shard_map/all_gather | solution.py:162
  416.6 5.5 %fusion.14 = f32[512,1408]{1,0:T(8,128)} fusion(bf16[512,1024]{1,0:T(8,128)(2,1)} %all-gather.2.cloned.1.call-done, bf16[2,1024,1408]{2,1,0:T(8,128)(2,1)} %param.42), kind=kOutput, calls=%fused_computation.37 | convolution fusion | flops 1476395008 | bytes 6815744 | tf_op jit(solution)/shard_map/dot_general | solution.py:163
  422.1 7.4 %convolution_convert_fusion = bf16[512,1024]{1,0:T(8,128)(2,1)} fusion(bf16[1408,1024]{1,0:T(8,128)(2,1)S(1)} %copy-done, bf16[512,1024]{1,0:T(8,128)(2,1)} %all-gather.2.cloned.1.call-done, bf16[2,1024,1408]{2,1,0:T(8,128)(2,1)} %param.42, f32[512,1408]{1,0:T(8,128)} %fusion.14), kind=kOutput, calls=%fused_computation.84 | convolution fusion | flops 2957639680 | bytes 10747904 | tf_op jit(solution)/shard_map/dot_general | solution.py:167
  429.6 15.2 %fusion.2 = f32[16,4,128,128]{3,2,1,0:T(8,128)} fusion(f32[16,4,128]{2,1,0:T(4,128)} %fusion.97, f32[16,4,128]{2,1,0:T(4,128)} %get-tuple-element.13, f32[16,4]{1,0:T(8,128)} %copy.275, f32[16,4,128]{2,1,0:T(4,128)} %fusion.98, f32[16,4,128]{2,1,0:T(4,128)} %get-tuple-element.20, f32[16,4]{1,0:T(8,128)} %copy.273, pred[16]{0:T(512)(128)(4,1)} %get-tuple-element.50, ...), kind=kLoop, calls=%fused_computation.7 | loop fusion | flops 41943040 | bytes 8915072 | tf_op jit(solution)/shard_map/jit(_where)/select_n | solution.py:187
  446.1 15.8 %add_select_fusion = f32[16,4,128,128]{3,2,1,0:T(8,128)} fusion(f32[16,4,128]{2,1,0:T(4,128)} %fusion.97, f32[16,4,128]{2,1,0:T(4,128)} %get-tuple-element.13, f32[16,4]{1,0:T(8,128)} %copy.275, f32[16,4,128]{2,1,0:T(4,128)} %fusion.98, f32[16,4,128,128]{3,2,1,0:T(8,128)} %copy-done.5, f32[16,4,128]{2,1,0:T(4,128)} %get-tuple-element.20, f32[16,4]{1,0:T(8,128)} %copy.273, ...), kind=kLoop, calls=%fused_computation.5 | loop fusion | flops 47185920 | bytes 13109888 | tf_op jit(solution)/shard_map/jit(_where)/select_n | solution.py:188
  461.9 2.0 fusion.80
  (218 shorter events, 57.5 us)
Async XLA Ops:
  7.2 414.9 %copy-start = (bf16[1408,1024]{1,0:T(8,128)(2,1)S(1)}, bf16[1408,1024]{1,0:T(8,128)(2,1)}, u32[]{:S(2)}) copy-start(bf16[1408,1024]{1,0:T(8,128)(2,1)} %param.43) | copy-start | bytes 8650756
  8.7 13.7 %all-to-all-start = ((s32[16,3,1]{1,2,0:T(1,128)}), s32[16,3,1]{1,2,0:T(1,128)S(1)}, u32[]{:S(2)}, u32[]{:S(2)}) async-start(s32[16,3,1]{1,2,0:T(1,128)} %bitcast.6), calls=%async_computation | async-start | bytes 16384 | tf_op jit(solution)/shard_map/all_to_all | solution.py:122
  22.4 20.1 %copy-start.48 = (s32[16,3,1]{1,2,0:T(1,128)}, s32[16,3,1]{1,2,0:T(1,128)S(1)}, u32[]{:S(2)}) copy-start(s32[16,3,1]{1,2,0:T(1,128)S(1)} %all-to-all-done) | copy-start | bytes 580
  22.4 20.2 %all-to-all-start.1 = ((s32[16,3,1]{1,2,0:T(1,128)}), s32[16,3,1]{1,2,0:T(1,128)S(1)}, u32[]{:S(2)}, u32[]{:S(2)}) async-start(s32[16,3,1]{1,2,0:T(1,128)} %bitcast.7), calls=%async_computation.1 | async-start | bytes 16384 | tf_op jit(solution)/shard_map/all_to_all | solution.py:123
  42.5 6.7 %copy-start.58 = (bf16[16,512]{1,0:T(8,128)(2,1)S(1)}, bf16[16,512]{1,0:T(8,128)(2,1)}, u32[]{:S(2)}) copy-start(bf16[16,512]{1,0:T(8,128)(2,1)} %param.29) | copy-start | bytes 49156
  42.5 7.3 %copy-start.59 = (bf16[16,512]{1,0:T(8,128)(2,1)S(1)}, bf16[16,512]{1,0:T(8,128)(2,1)}, u32[]{:S(2)}) copy-start(bf16[16,512]{1,0:T(8,128)(2,1)} %param.28) | copy-start | bytes 49156
  42.6 8.8 %copy-start.70 = (f32[1024]{0:T(1024)S(1)}, f32[1024]{0:T(1024)}, u32[]{:S(2)}) copy-start(f32[1024]{0:T(1024)} %param.23) | copy-start | bytes 12292
  43.2 229.8 %all-to-all-start.2 = ((bf16[48,2,128,512]{2,3,1,0:T(8,128)(2,1)}), bf16[48,2,128,512]{2,3,1,0:T(8,128)(2,1)}, u32[]{:S(2)}, u32[]{:S(2)}) async-start(bf16[48,2,128,512]{2,3,1,0:T(8,128)(2,1)} %copy.234), calls=%async_computation.2 | async-start | bytes 25165824 | tf_op jit(solution)/shard_map/all_to_all | solution.py:121
  49.2 342.6 %reduce-scatter.3.cloned.1.call-start = ((), (), s32[]{:S(2)}) async-start(), calls=%async_computation.5 | async-start | bytes 1572864 | tf_op jit(solution)/shard_map/reduce_scatter | solution.py:153
  58.8 11.6 %copy-start.68 = (s32[16,8]{0,1:T(8,128)S(1)}, s32[16,8]{0,1:T(8,128)}, u32[]{:S(2)}) copy-start(s32[16,8]{0,1:T(8,128)} %param.35) | copy-start | bytes 1540
  90.8 9.2 %copy-start.18 = (f32[16,8,4,128]{3,2,1,0:T(4,128)S(1)}, f32[16,8,4,128]{3,2,1,0:T(4,128)}, u32[]{:S(2)}) copy-start(f32[16,8,4,128]{3,2,1,0:T(4,128)} %convert.1) | copy-start | bytes 786436
  90.8 9.2 %copy-start.1 = (f32[16,4,128,128]{3,2,1,0:T(8,128)S(1)}, f32[16,4,128,128]{3,2,1,0:T(8,128)}, u32[]{:S(2)}) copy-start(f32[16,4,128,128]{3,2,1,0:T(8,128)} %param.38) | copy-start | bytes 12582916
  90.8 9.2 %copy-start.44 = (f32[16,4]{1,0:T(8,128)S(1)}, f32[16,4]{1,0:T(8,128)}, u32[]{:S(2)}) copy-start(f32[16,4]{1,0:T(8,128)} %copy.259) | copy-start | bytes 772
  92.9 41.3 %copy-start.52 = (pred[16]{0:T(512)(128)(4,1)}, pred[16]{0:T(512)(128)(4,1)S(1)}, u32[]{:S(2)}) copy-start(pred[16]{0:T(512)(128)(4,1)S(1)} %get-tuple-element.52) | copy-start | bytes 52
  92.9 41.3 %copy-start.54 = (pred[16]{0:T(512)(128)(4,1)}, pred[16]{0:T(512)(128)(4,1)S(1)}, u32[]{:S(2)}) copy-start(pred[16]{0:T(512)(128)(4,1)S(1)} %get-tuple-element.46) | copy-start | bytes 52
  92.9 41.3 %copy-start.56 = (pred[16]{0:T(512)(128)(4,1)}, pred[16]{0:T(512)(128)(4,1)S(1)}, u32[]{:S(2)}) copy-start(pred[16]{0:T(512)(128)(4,1)S(1)} %get-tuple-element.47) | copy-start | bytes 52
  92.9 47.1 %copy-start.60 = (pred[16]{0:T(512)(128)(4,1)}, pred[16]{0:T(512)(128)(4,1)S(1)}, u32[]{:S(2)}) copy-start(pred[16]{0:T(512)(128)(4,1)S(1)} %get-tuple-element.48) | copy-start | bytes 52
  94.5 39.7 %copy-start.9 = (f32[16,4,128]{2,1,0:T(4,128)}, f32[16,4,128]{2,1,0:T(4,128)S(1)}, u32[]{:S(2)}) copy-start(f32[16,4,128]{2,1,0:T(4,128)S(1)} %get-tuple-element.16) | copy-start | bytes 98308
  94.5 39.7 %copy-start.11 = (f32[16,4,128]{2,1,0:T(4,128)}, f32[16,4,128]{2,1,0:T(4,128)S(1)}, u32[]{:S(2)}) copy-start(f32[16,4,128]{2,1,0:T(4,128)S(1)} %get-tuple-element.17) | copy-start | bytes 98308
  94.5 45.5 %copy-start.19 = (f32[16,4,128]{2,1,0:T(4,128)}, f32[16,4,128]{2,1,0:T(4,128)S(1)}, u32[]{:S(2)}) copy-start(f32[16,4,128]{2,1,0:T(4,128)S(1)} %get-tuple-element.18) | copy-start | bytes 98308
  100.0 6.7 %copy-start.2 = (f32[16,4,128,128]{3,2,1,0:T(8,128)S(1)}, f32[16,4,128,128]{3,2,1,0:T(8,128)}, u32[]{:S(2)}) copy-start(f32[16,4,128,128]{3,2,1,0:T(8,128)} %param.37) | copy-start | bytes 12582916
  100.0 6.7 %copy-start.28 = (f32[16,4]{1,0:T(8,128)S(1)}, f32[16,4]{1,0:T(8,128)}, u32[]{:S(2)}) copy-start(f32[16,4]{1,0:T(8,128)} %copy.263) | copy-start | bytes 772
  100.0 6.7 %copy-start.47 = (f32[16,4]{1,0:T(8,128)S(1)}, f32[16,4]{1,0:T(8,128)}, u32[]{:S(2)}) copy-start(f32[16,4]{1,0:T(8,128)} %copy.258) | copy-start | bytes 772
  113.9 20.2 %copy-start.13 = (f32[16,4,128]{2,1,0:T(4,128)}, f32[16,4,128]{2,1,0:T(4,128)S(1)}, u32[]{:S(2)}) copy-start(f32[16,4,128]{2,1,0:T(4,128)S(1)} %fusion.102) | copy-start | bytes 98308
  114.0 8.0 %copy-start.32 = (f32[16,4]{1,0:T(8,128)S(1)}, f32[16,4]{1,0:T(8,128)}, u32[]{:S(2)}) copy-start(f32[16,4]{1,0:T(8,128)} %copy.267) | copy-start | bytes 772
  114.0 8.0 %copy-start.51 = (f32[16,4]{1,0:T(8,128)S(1)}, f32[16,4]{1,0:T(8,128)}, u32[]{:S(2)}) copy-start(f32[16,4]{1,0:T(8,128)} %copy.256) | copy-start | bytes 772
  122.0 12.2 %copy-start.15 = (f32[16,4,128]{2,1,0:T(4,128)}, f32[16,4,128]{2,1,0:T(4,128)S(1)}, u32[]{:S(2)}) copy-start(f32[16,4,128]{2,1,0:T(4,128)S(1)} %fusion.101) | copy-start | bytes 98308
  128.4 11.6 %copy-start.4 = (f32[16,4,128,128]{3,2,1,0:T(8,128)}, f32[16,4,128,128]{3,2,1,0:T(8,128)S(1)}, u32[]{:S(2)}) copy-start(f32[16,4,128,128]{3,2,1,0:T(8,128)S(1)} %add_select_fusion.4) | copy-start | bytes 12582916
  132.1 7.9 %copy-start.21 = (f32[16,4,128]{2,1,0:T(4,128)}, f32[16,4,128]{2,1,0:T(4,128)S(1)}, u32[]{:S(2)}) copy-start(f32[16,4,128]{2,1,0:T(4,128)S(1)} %fusion.100) | copy-start | bytes 98308
  134.2 7.8 %copy-start.36 = (f32[16,4]{1,0:T(8,128)S(1)}, f32[16,4]{1,0:T(8,128)}, u32[]{:S(2)}) copy-start(f32[16,4]{1,0:T(8,128)} %copy.269) | copy-start | bytes 772
  134.2 7.8 %copy-start.45 = (f32[16,4]{1,0:T(8,128)S(1)}, f32[16,4]{1,0:T(8,128)}, u32[]{:S(2)}) copy-start(f32[16,4]{1,0:T(8,128)} %copy.255) | copy-start | bytes 772
  272.9 8.6 %copy-start.8 = (bf16[48,32,512]{2,1,0:T(8,128)(2,1)S(1)}, bf16[48,32,512]{2,1,0:T(8,128)(2,1)}, u32[]{:S(2)}) copy-start(bf16[48,32,512]{2,1,0:T(8,128)(2,1)} %gather_fusion) | copy-start | bytes 4718596
  272.9 8.6 %copy-start.43 = (pred[48,128]{1,0:T(8,128)(4,1)S(1)}, pred[48,128]{1,0:T(8,128)(4,1)}, u32[]{:S(2)}) copy-start(pred[48,128]{1,0:T(8,128)(4,1)} %add_compare_fusion) | copy-start | bytes 18436
  320.3 5.4 %copy-start.10 = (f32[16,4,128]{2,1,0:T(4,128)S(1)}, f32[16,4,128]{2,1,0:T(4,128)}, u32[]{:S(2)}) copy-start(f32[16,4,128]{2,1,0:T(4,128)} %copy-done.9) | copy-start | bytes 98308
  320.3 5.4 %copy-start.12 = (f32[16,4,128]{2,1,0:T(4,128)S(1)}, f32[16,4,128]{2,1,0:T(4,128)}, u32[]{:S(2)}) copy-start(f32[16,4,128]{2,1,0:T(4,128)} %copy-done.11) | copy-start | bytes 98308
  320.4 5.4 %copy-start.14 = (f32[16,4,128]{2,1,0:T(4,128)S(1)}, f32[16,4,128]{2,1,0:T(4,128)}, u32[]{:S(2)}) copy-start(f32[16,4,128]{2,1,0:T(4,128)} %copy-done.13) | copy-start | bytes 98308
  320.4 5.4 %copy-start.16 = (f32[16,4,128]{2,1,0:T(4,128)S(1)}, f32[16,4,128]{2,1,0:T(4,128)}, u32[]{:S(2)}) copy-start(f32[16,4,128]{2,1,0:T(4,128)} %copy-done.15) | copy-start | bytes 98308
  320.4 5.4 %copy-start.20 = (f32[16,4,128]{2,1,0:T(4,128)S(1)}, f32[16,4,128]{2,1,0:T(4,128)}, u32[]{:S(2)}) copy-start(f32[16,4,128]{2,1,0:T(4,128)} %copy-done.19) | copy-start | bytes 98308
  320.4 5.4 %copy-start.22 = (f32[16,4,128]{2,1,0:T(4,128)S(1)}, f32[16,4,128]{2,1,0:T(4,128)}, u32[]{:S(2)}) copy-start(f32[16,4,128]{2,1,0:T(4,128)} %copy-done.21) | copy-start | bytes 98308
  320.4 5.4 %copy-start.26 = (f32[16,4,128]{2,1,0:T(4,128)S(1)}, f32[16,4,128]{2,1,0:T(4,128)}, u32[]{:S(2)}) copy-start(f32[16,4,128]{2,1,0:T(4,128)} %get-tuple-element.19) | copy-start | bytes 98308
  320.4 5.4 %copy-start.29 = (f32[16,4]{1,0:T(8,128)S(1)}, f32[16,4]{1,0:T(8,128)}, u32[]{:S(2)}) copy-start(f32[16,4]{1,0:T(8,128)} %copy.263) | copy-start | bytes 772
  320.4 5.4 %copy-start.31 = (f32[16,4]{1,0:T(8,128)S(1)}, f32[16,4]{1,0:T(8,128)}, u32[]{:S(2)}) copy-start(f32[16,4]{1,0:T(8,128)} %copy.265) | copy-start | bytes 772
  320.4 5.4 %copy-start.33 = (f32[16,4]{1,0:T(8,128)S(1)}, f32[16,4]{1,0:T(8,128)}, u32[]{:S(2)}) copy-start(f32[16,4]{1,0:T(8,128)} %copy.267) | copy-start | bytes 772
  322.7 93.9 %all-gather.2.cloned.1.call-start = ((), (), s32[]{:S(2)}) async-start(), calls=%async_computation.6 | async-start | bytes 1572864 | tf_op jit(solution)/shard_map/all_gather | solution.py:162
  323.5 12.7 %copy-start.27 = (f32[16,4,128]{2,1,0:T(4,128)}, f32[16,4,128]{2,1,0:T(4,128)S(1)}, u32[]{:S(2)}) copy-start(f32[16,4,128]{2,1,0:T(4,128)S(1)} %fusion.99) | copy-start | bytes 98308
  323.6 12.6 %copy-start.42 = (f32[16,4]{1,0:T(8,128)}, f32[16,4]{1,0:T(8,128)S(1)}, u32[]{:S(2)}) copy-start(f32[16,4]{1,0:T(8,128)S(1)} %copy.271) | copy-start | bytes 772
  325.9 12.4 %copy-start.38 = (f32[16,1,4,128]{3,2,1,0:T(4,128)S(1)}, f32[16,1,4,128]{3,2,1,0:T(4,128)}, u32[]{:S(2)}) copy-start(f32[16,1,4,128]{3,2,1,0:T(4,128)} %get-tuple-element.22) | copy-start | bytes 98308
  395.0 66.9 %reduce-scatter.5.cloned.1.call-start = ((), (), s32[]{:S(2)}) async-start(), calls=%async_computation.7 | async-start | bytes 1572864 | tf_op jit(solution)/shard_map/reduce_scatter | solution.py:166
  (29 other events, 113.4 us)
Sparse Core Ops, SparseCore 0:
  322.8 68.9 reduce-scatter.2
  395.1 21.4 all-gather.1
  429.7 20.3 reduce-scatter.4
where the time goes:
time: 478 us; the launch traced here: 471 us
  waiting for transfers between devices  176 us (37%)
  matrix products  96.6 us (20%)
  other arithmetic  91.4 us (19%)
  local copies, waits for them, and re-layouts  74.8 us (16%)
  starting transfers between devices  17 us (4%)
  between operations  15 us (3%)
    all_to_all x1, waiting for transfers between devices, on_device(): lax.all_to_all(kv_cache, 'req', split_axis=0, concat_axis=0, tiled=True)  111 us
    reduce_scatter x1, waiting for transfers between devices, on_device(): lax.psum_scatter(jnp.dot(mixed, w_out, preferred_element_type=jnp.float32...  48.5 us
    dot_general x8, matrix products, on_device(): jnp.einsum('rhd,rhde->rhe', unit, memory, precision=lax.Precision.HIGHEST)  45.1 us
    select_n x4, other arithmetic, on_device(): memory = jnp.where(live, new_mem, memory)  36 us
    unnamed x143, local copies, waits for them, and re-layouts  21.6 us
    select_n x2, other arithmetic, on_device(): momentum = jnp.where(live, new_mom, momentum)  20.9 us
    all_gather x1, waiting for transfers between devices, on_device(): piece = lax.all_gather(ffn_in, 'grp', axis=0, tiled=True)  11 us
  transfers between devices with their start and end apart: 6, of which 4 were waited for; matrix products, arithmetic and copies ran while one was open for 40% of the time, Pallas kernels for 0%

commit v1 on v0

--- a/solution.py
+++ b/solution.py
@@ -1,3 +1,4 @@
+import functools
 import math
 import jax
 import jax.numpy as jnp
@@ -8,6 +9,37 @@
 EPS = 1e-06
 THETA = 0.5
 NEG = -1e30
+
+
+def assign_the_desk(array_here, ndim_at, frame):
+    carry = array_here.shape
+    extra = array_here.reshape(
+        *carry[:ndim_at], frame, carry[ndim_at] // frame, *carry[ndim_at + 1 :]
+    )
+    return jnp.moveaxis(extra, ndim_at, 0)
+
+
+def _number_loops(inp, dim_i):
+    inp = jnp.moveaxis(inp, 0, dim_i)
+    y_new = inp.shape
+    return inp.reshape(*y_new[:dim_i], y_new[dim_i] * y_new[dim_i + 1], *y_new[dim_i + 2 :])
+
+
+def trace_the_sector(arr_in, link_axis, piece_in, point):
+    d_next, part_next = (jax.lax.psum(1, link_axis), jax.lax.axis_index(link_axis))
+    k_now = assign_the_desk(arr_in, piece_in, d_next)
+    newest = k_now
+    for tick in range(1, d_next):
+        r1, vec_out = ((part_next + tick) % d_next, (part_next - tick) % d_next)
+        e_next = lax.dynamic_index_in_dim(k_now, r1, 0)
+        y2 = jax.lax.ppermute(
+            e_next, link_axis, list(map(lambda m: (m, (m + tick) % d_next), range(d_next)))
+        )
+        newest = lax.dynamic_update_slice_in_dim(newest, y2, vec_out, axis=0)
+    return _number_loops(newest, point)
+
+
+wait_scenes = functools.partial(trace_the_sector, link_axis="req", piece_in=0, point=0)
 
 
 def rms_norm(rows, gain):
@@ -119,7 +151,7 @@
     request_ids = jnp.arange(reqs, dtype=jnp.int32)
     moved_pages, moved_request, moved_page = (
         lax.all_to_all(kv_cache, "req", split_axis=0, concat_axis=0, tiled=True),
-        lax.all_to_all(slot_request, "req", split_axis=0, concat_axis=0, tiled=True),
+        wait_scenes(slot_request),
         lax.all_to_all(slot_page, "req", split_axis=0, concat_axis=0, tiled=True),
     )
     local_request = moved_request - first_request

time: 478 us -> 514 us (1.075)
  starting transfers between devices: 17 us -> 96.6 us
  waiting for transfers between devices: 176 us -> 115 us
  local copies, waits for them, and re-layouts: 74.8 us -> 91.1 us
    all_to_all x1, waiting for transfers between devices: 111 us -> 0.01 us  [on_device(): lax.all_to_all(kv_cache, 'req', split_axis=0, concat_axis=0, tiled=True)]
    ppermute x0 -> x15, waiting for transfers between devices: none -> 105 us  [trace_the_sector(): jax.lax.ppermute(e_next, link_axis, list(map(lambda m: (m, (m + tick) % d...]
    ppermute x0 -> x15, starting transfers between devices: none -> 83.1 us  [trace_the_sector(): jax.lax.ppermute(e_next, link_axis, list(map(lambda m: (m, (m + tick) % d...]
    reduce_scatter x1, waiting for transfers between devices: 48.5 us -> 0.01 us  [on_device(): lax.psum_scatter(jnp.dot(mixed, w_out, preferred_element_type=jnp.float32...]
    dynamic_update_slice x0 -> x15, local copies, waits for them, and re-layouts: none -> 19.2 us  [trace_the_sector(): newest = lax.dynamic_update_slice_in_dim(newest, y2, vec_out, axis=0)]
    all_to_all x1 -> x0, starting transfers between devices: 7.39 us -> none  [on_device(): lax.all_to_all(slot_request, 'req', split_axis=0, concat_axis=0, tiled=True)]
    unnamed x143 -> x147, local copies, waits for them, and re-layouts: 21.6 us -> 19.6 us
  transfers between devices with their start and end apart: 6 -> 20, of which waited for: 4 -> 2; matrix products, arithmetic and copies ran while one was open for 40% -> 41% of each run, Pallas kernels for 0% -> 0%
where the time goes in v1:
time: 514 us; the launch traced here: 505 us
  waiting for transfers between devices  115 us (22%)
  matrix products  96.7 us (19%)
  starting transfers between devices  96.6 us (19%)
  local copies, waits for them, and re-layouts  91.1 us (18%)
  other arithmetic  90.3 us (18%)
  between operations  15.3 us (3%)
    ppermute x15, waiting for transfers between devices, trace_the_sector(): jax.lax.ppermute(e_next, link_axis, list(map(lambda m: (m, (m + tick) % d...  105 us
    ppermute x15, starting transfers between devices, trace_the_sector(): jax.lax.ppermute(e_next, link_axis, list(map(lambda m: (m, (m + tick) % d...  83.1 us
    dot_general x8, matrix products, on_device(): jnp.einsum('rhd,rhde->rhe', unit, memory, precision=lax.Precision.HIGHEST)  45.1 us
    select_n x4, other arithmetic, on_device(): memory = jnp.where(live, new_mem, memory)  36 us
    select_n x2, other arithmetic, on_device(): momentum = jnp.where(live, new_mom, momentum)  20.9 us
    unnamed x147, local copies, waits for them, and re-layouts  19.6 us
    dynamic_update_slice x15, local copies, waits for them, and re-layouts, trace_the_sector(): newest = lax.dynamic_update_slice_in_dim(newest, y2, vec_out, axis=0)  19.2 us
  transfers between devices with their start and end apart: 20, of which 2 were waited for; matrix products, arithmetic and copies ran while one was open for 41% of the time, Pallas kernels for 0%

profile of v1, /device:TPU:0, one launch (start us, length us, event | category | flops | bytes accessed | tf_op | source)
XLA Modules:
  0.0 505.4 jit_solution(16400865061872435402)
XLA Ops:
  8.7 7.4 %all-to-all-start = ((s32[16,3,1]{1,2,0:T(1,128)}), s32[16,3,1]{1,2,0:T(1,128)S(1)}, u32[]{:S(2)}, u32[]{:S(2)}) async-start(s32[16,3,1]{1,2,0:T(1,128)} %bitcast.6), calls=%async_computation | async-start | bytes 16384 | tf_op jit(solution)/shard_map/all_to_all | solution.py:155
  16.1 16.7 %copy.231 = bf16[48,2,128,512]{2,3,1,0:T(8,128)(2,1)} copy(bf16[48,2,128,512]{3,2,1,0:T(8,128)(2,1)} %param.30) | data formatting | bytes 25165824 | tf_op args[8]
  33.4 6.0 %all-to-all-start.1 = ((bf16[48,2,128,512]{2,3,1,0:T(8,128)(2,1)}), bf16[48,2,128,512]{2,3,1,0:T(8,128)(2,1)}, u32[]{:S(2)}, u32[]{:S(2)}) async-start(bf16[48,2,128,512]{2,3,1,0:T(8,128)(2,1)} %copy.231), calls=%async_computation.1 | async-start | bytes 25165824 | tf_op jit(solution)/shard_map/all_to_all | solution.py:153
  42.6 2.2 collective-permute-start.2
  48.6 3.1 convolution_convert_fusion.4
  52.9 3.1 convolution_convert_fusion.3
  56.0 2.0 reshape.252
  57.9 2.2 fusion.142
  60.1 2.4 copy.223
  62.5 3.1 convolution_convert_fusion.2
  65.6 2.0 reshape.254
  67.8 2.0 gather_fusion.1
  69.7 2.6 gather_fusion.2
  91.7 5.5 %fusion.144 = f32[16,4,1,128]{3,2,1,0:T(1,128)S(1)} fusion(f32[16,4,128,1]{2,3,1,0:T(1,128)S(1)} %bitcast.260, f32[16,4,128,128]{3,2,1,0:T(8,128)} %param.37), kind=kOutput, calls=%fused_computation.249 | convolution fusion | flops 12582912 | bytes 4259840 | tf_op jit(solution)/shard_map/rhd,rhde->rhe/dot_general | solution.py:212
  97.2 6.6 %fusion.36 = f32[16,4,1,128]{3,2,1,0:T(1,128)S(1)} fusion(f32[16,4,128,1]{2,3,1,0:T(1,128)S(1)} %bitcast.259, f32[16,4,128,128]{3,2,1,0:T(8,128)} %param.37, f32[16,4,128,128]{3,2,1,0:T(8,128)S(1)} %copy-done.1, f32[16,4,128]{2,1,0:T(4,128)S(1)} %fusion.104, f32[16,4,128]{2,1,0:T(4,128)S(1)} %get-tuple-element.12, f32[16,4]{1,0:T(8,128)S(1)} %copy.257, ...), kind=kOutput, calls=%fused_computation.61 | convolution fusion | flops 19922944 | bytes 8520208 | tf_op jit(solution)/shard_map/rhd,rhde->rhe/dot_general | solution.py:212
  103.9 3.6 add_select_fusion.6
  107.5 3.7 fusion.145
  111.2 7.9 %fusion.30 = f32[16,4,1,128]{3,2,1,0:T(1,128)S(1)} fusion(f32[16,4,128,1]{2,3,1,0:T(1,128)S(1)} %bitcast.269, f32[16,4,128,128]{3,2,1,0:T(8,128)S(1)} %add_select_fusion.6, f32[16,4,128]{2,1,0:T(4,128)S(1)} %fusion.102, f32[16,4,128]{2,1,0:T(4,128)S(1)} %get-tuple-element.14, f32[16,4]{1,0:T(8,128)S(1)} %copy-done.30, f32[16,4]{1,0:T(8,128)S(1)} %copy-done.50, ...), kind=kOutput, calls=%fused_computation.55 | convolution fusion | flops 30408704 | bytes 8651824 | tf_op jit(solution)/shard_map/rhd,rhde->rhe/dot_general | solution.py:212
  119.2 6.4 %add_select_fusion.4 = f32[16,4,128,128]{3,2,1,0:T(8,128)S(1)} fusion(f32[16,4,128]{2,1,0:T(4,128)S(1)} %fusion.101, f32[16,4,128]{2,1,0:T(4,128)S(1)} %get-tuple-element.15, f32[16,4]{1,0:T(8,128)S(1)} %copy-done.32, f32[16,4,128]{2,1,0:T(4,128)S(1)} %fusion.102, f32[16,4,128,128]{3,2,1,0:T(8,128)S(1)} %add_select_fusion.6, ...), kind=kLoop, calls=%fused_computation.17 | loop fusion | flops 26214400 | bytes 12846656 | tf_op jit(solution)/shard_map/jit(_where)/select_n | solution.py:220
  125.7 3.6 fusion.146
  129.4 2.0 fusion.143
  131.5 5.7 %fusion.6 = f32[16,4,128,128]{3,2,1,0:T(8,128)S(1)} fusion(f32[16,4,128]{2,1,0:T(4,128)S(1)} %fusion.101, f32[16,4,128]{2,1,0:T(4,128)S(1)} %get-tuple-element.15, f32[16,4]{1,0:T(8,128)S(1)} %copy-done.32, f32[16,4,128]{2,1,0:T(4,128)S(1)} %fusion.102, f32[16,4,128]{2,1,0:T(4,128)S(1)} %get-tuple-element.14, f32[16,4]{1,0:T(8,128)S(1)} %copy-done.30, ...), kind=kLoop, calls=%fused_computation.19 | loop fusion | flops 20971520 | bytes 8651840 | tf_op jit(solution)/shard_map/jit(_where)/select_n | solution.py:219
  137.3 4.9 fusion.27
  142.2 105.2 %collective-permute-done = s32[1,3]{1,0:T(1,128)} collective-permute-done((s32[1,3]{1,0:T(1,128)}, s32[1,3]{1,0:T(1,128)}, u32[]{:S(2)}, u32[]{:S(2)}) %collective-permute-start) | collective-permute-done | bytes 44 | tf_op jit(solution)/shard_map/ppermute | solution.py:35
  248.7 64.6 %collective-permute-start.6 = (s32[1,3]{1,0:T(1,128)}, s32[1,3]{1,0:T(1,128)}, u32[]{:S(2)}, u32[]{:S(2)}) collective-permute-start(s32[1,3]{1,0:T(1,128)} %get-tuple-element.51), channel_id=1, source_target_pairs={{0,14},{2,16},{4,18},{6,20},{8,22},{10,24},{12,26},{14,28},{16,30}... | collective-permute-start | bytes 44 | tf_op jit(solution)/shard_map/ppermute | solution.py:35
  314.6 2.2 collective-permute-start.7
  318.1 2.4 collective-permute-start.8
  321.7 3.8 collective-permute-start.9
  328.1 2.4 collective-permute-start.11
  348.5 3.0 gather_fusion
  357.3 8.8 %fusion.141 = (bf16[48,1,128,512]{2,3,1,0:T(8,128)(2,1)}, bf16[48,1,128,512]{2,3,1,0:T(8,128)(2,1)S(1)}) fusion(bf16[48,2,128,512]{2,3,1,0:T(8,128)(2,1)} %all-to-all-done.1), kind=kLoop, calls=%fused_computation.246 | loop fusion | bytes 25165824 | tf_op jit(solution)/shard_map/slice | solution.py:63
  366.1 4.1 fusion.18
  378.3 4.1 fusion.19
  382.4 5.9 %bitcast_multiply_fusion = f32[48,32,4,128]{3,1,2,0:T(8,128)S(1)} fusion(bf16[48,128,4,128]{1,3,2,0:T(8,128)(2,1)} %bitcast.247, f32[48,4,32,128]{3,2,1,0:T(8,128)S(1)} %copy-done.6, f32[48,32,4]{1,2,0:T(4,128)} %copy.241, f32[48,4,32]{2,1,0:T(4,128)} %get-tuple-element.66, pred[48,128]{1,0:T(8,128)(4,1)} %add_compare_fusion), kind=kOutput, calls=%fused_computation.30 | convolution fusion | flops 206045184 | bytes 12638208 | tf_op jit(solution)/shard_map/shit,sthd->sihd/dot_general | solution.py:74
  388.3 4.7 fusion.10
  394.6 2.6 fusion.93
  400.4 3.9 fusion.70
  405.0 1.8 convolution_convert_fusion.1
  410.0 10.3 %add_select_fusion.2 = f32[16,4,128,128]{3,2,1,0:T(8,128)S(1)} fusion(f32[16,4,128]{2,1,0:T(4,128)S(1)} %fusion.99, f32[16,4,128]{2,1,0:T(4,128)S(1)} %copy-done.26, f32[16,4]{1,0:T(8,128)S(1)} %copy.268, f32[16,4,128]{2,1,0:T(4,128)S(1)} %copy-done.22, f32[16,4,128,128]{3,2,1,0:T(8,128)} %copy-done.4, f32[16,4,128]{2,1,0:T(4,128)S(1)} %copy-done.20, ...), kind=kLoop, calls=%fused_computation.11 | loop fusion | flops 36700160 | bytes 12978272 | tf_op jit(solution)/shard_map/jit(_where)/select_n | solution.py:220
  420.4 2.0 copy-done.5
  422.4 3.7 fusion.147
  430.6 9.2 %fusion.24 = f32[16,4,1,128]{3,2,1,0:T(1,128)S(1)} fusion(f32[16,4,128,1]{2,3,1,0:T(1,128)} %bitcast.268, f32[16,4,128,128]{3,2,1,0:T(8,128)} %copy-done.5, f32[16,4,128]{2,1,0:T(4,128)} %fusion.98, f32[16,4,128]{2,1,0:T(4,128)} %get-tuple-element.18, f32[16,4]{1,0:T(8,128)} %copy.270, f32[16,4]{1,0:T(8,128)} %copy.250, ...), kind=kOutput, calls=%fused_computation.49 | convolution fusion | flops 30408704 | bytes 8651824 | tf_op jit(solution)/shard_map/rhd,rhde->rhe/dot_general | solution.py:212
  441.2 10.0 %all-gather.2.cloned.1.call-done = bf16[512,1024]{1,0:T(8,128)(2,1)} async-done(((bf16[256,1024]{1,0:T(8,128)(2,1)}), bf16[512,1024]{1,0:T(8,128)(2,1)}) %all-gather.2.cloned.1.call-update) | async-done | bytes 1048592 | tf_op jit(solution)/shard_map/all_gather | solution.py:194
  451.3 5.5 %fusion.14 = f32[512,1408]{1,0:T(8,128)} fusion(bf16[512,1024]{1,0:T(8,128)(2,1)} %all-gather.2.cloned.1.call-done, bf16[2,1024,1408]{2,1,0:T(8,128)(2,1)} %param.42), kind=kOutput, calls=%fused_computation.37 | convolution fusion | flops 1476395008 | bytes 6815744 | tf_op jit(solution)/shard_map/dot_general | solution.py:195
  456.8 7.5 %convolution_convert_fusion = bf16[512,1024]{1,0:T(8,128)(2,1)} fusion(bf16[1408,1024]{1,0:T(8,128)(2,1)S(1)} %copy-done, bf16[512,1024]{1,0:T(8,128)(2,1)} %all-gather.2.cloned.1.call-done, bf16[2,1024,1408]{2,1,0:T(8,128)(2,1)} %param.42, f32[512,1408]{1,0:T(8,128)} %fusion.14), kind=kOutput, calls=%fused_computation.84 | convolution fusion | flops 2957639680 | bytes 10747904 | tf_op jit(solution)/shard_map/dot_general | solution.py:199
  464.3 15.2 %fusion.2 = f32[16,4,128,128]{3,2,1,0:T(8,128)} fusion(f32[16,4,128]{2,1,0:T(4,128)} %fusion.97, f32[16,4,128]{2,1,0:T(4,128)} %get-tuple-element.11, f32[16,4]{1,0:T(8,128)} %copy.272, f32[16,4,128]{2,1,0:T(4,128)} %fusion.98, f32[16,4,128]{2,1,0:T(4,128)} %get-tuple-element.18, f32[16,4]{1,0:T(8,128)} %copy.270, pred[16]{0:T(512)(128)(4,1)} %get-tuple-element.63, ...), kind=kLoop, calls=%fused_computation.7 | loop fusion | flops 41943040 | bytes 8915072 | tf_op jit(solution)/shard_map/jit(_where)/select_n | solution.py:219
  480.8 15.8 %add_select_fusion = f32[16,4,128,128]{3,2,1,0:T(8,128)} fusion(f32[16,4,128]{2,1,0:T(4,128)} %fusion.97, f32[16,4,128]{2,1,0:T(4,128)} %get-tuple-element.11, f32[16,4]{1,0:T(8,128)} %copy.272, f32[16,4,128]{2,1,0:T(4,128)} %fusion.98, f32[16,4,128,128]{3,2,1,0:T(8,128)} %copy-done.5, f32[16,4,128]{2,1,0:T(4,128)} %get-tuple-element.18, f32[16,4]{1,0:T(8,128)} %copy.270, ...), kind=kLoop, calls=%fused_computation.5 | loop fusion | flops 47185920 | bytes 13109888 | tf_op jit(solution)/shard_map/jit(_where)/select_n | solution.py:220
  496.6 2.0 fusion.80
  (265 shorter events, 84.7 us)
Async XLA Ops:
  7.2 449.6 %copy-start = (bf16[1408,1024]{1,0:T(8,128)(2,1)S(1)}, bf16[1408,1024]{1,0:T(8,128)(2,1)}, u32[]{:S(2)}) copy-start(bf16[1408,1024]{1,0:T(8,128)(2,1)} %param.43) | copy-start | bytes 8650756
  8.7 24.1 %all-to-all-start = ((s32[16,3,1]{1,2,0:T(1,128)}), s32[16,3,1]{1,2,0:T(1,128)S(1)}, u32[]{:S(2)}, u32[]{:S(2)}) async-start(s32[16,3,1]{1,2,0:T(1,128)} %bitcast.6), calls=%async_computation | async-start | bytes 16384 | tf_op jit(solution)/shard_map/all_to_all | solution.py:155
  32.7 13.7 %copy-start.58 = (bf16[16,512]{1,0:T(8,128)(2,1)S(1)}, bf16[16,512]{1,0:T(8,128)(2,1)}, u32[]{:S(2)}) copy-start(bf16[16,512]{1,0:T(8,128)(2,1)} %param.29) | copy-start | bytes 49156
  32.8 14.3 %copy-start.59 = (bf16[16,512]{1,0:T(8,128)(2,1)S(1)}, bf16[16,512]{1,0:T(8,128)(2,1)}, u32[]{:S(2)}) copy-start(bf16[16,512]{1,0:T(8,128)(2,1)} %param.28) | copy-start | bytes 49156
  32.8 15.8 %copy-start.72 = (f32[1024]{0:T(1024)S(1)}, f32[1024]{0:T(1024)}, u32[]{:S(2)}) copy-start(f32[1024]{0:T(1024)} %param.23) | copy-start | bytes 12292
  33.4 323.9 %all-to-all-start.1 = ((bf16[48,2,128,512]{2,3,1,0:T(8,128)(2,1)}), bf16[48,2,128,512]{2,3,1,0:T(8,128)(2,1)}, u32[]{:S(2)}, u32[]{:S(2)}) async-start(bf16[48,2,128,512]{2,3,1,0:T(8,128)(2,1)} %copy.231), calls=%async_computation.1 | async-start | bytes 25165824 | tf_op jit(solution)/shard_map/all_to_all | solution.py:153
  39.4 388.0 %reduce-scatter.3.cloned.1.call-start = ((), (), s32[]{:S(2)}) async-start(), calls=%async_computation.4 | async-start | bytes 1572864 | tf_op jit(solution)/shard_map/reduce_scatter | solution.py:185
  39.7 8.8 %copy-start.47 = (s32[16,3]{1,0:T(8,128)}, s32[16,3]{1,0:T(8,128)S(1)}, u32[]{:S(2)}) copy-start(s32[16,3]{1,0:T(8,128)S(1)} %reshape.255) | copy-start | bytes 580
  40.5 206.9 %collective-permute-start = (s32[1,3]{1,0:T(1,128)}, s32[1,3]{1,0:T(1,128)}, u32[]{:S(2)}, u32[]{:S(2)}) collective-permute-start(s32[1,3]{1,0:T(1,128)} %get-tuple-element.57), channel_id=1, source_target_pairs={{0,2},{2,4},{4,6},{6,8},{8,10},{10,12},{12,14},{14,16},{16,18},{18... | collective-permute-start | bytes 44 | tf_op jit(solution)/shard_map/ppermute | solution.py:35
  40.9 207.7 %collective-permute-start.1 = (s32[1,3]{1,0:T(1,128)}, s32[1,3]{1,0:T(1,128)}, u32[]{:S(2)}, u32[]{:S(2)}) collective-permute-start(s32[1,3]{1,0:T(1,128)} %get-tuple-element.56), channel_id=1, source_target_pairs={{0,4},{2,6},{4,8},{6,10},{8,12},{10,14},{12,16},{14,18},{16,20},{1... | collective-permute-start | bytes 44 | tf_op jit(solution)/shard_map/ppermute | solution.py:35
  42.6 272.0 %collective-permute-start.2 = (s32[1,3]{1,0:T(1,128)}, s32[1,3]{1,0:T(1,128)}, u32[]{:S(2)}, u32[]{:S(2)}) collective-permute-start(s32[1,3]{1,0:T(1,128)} %get-tuple-element.55), channel_id=1, source_target_pairs={{0,6},{2,8},{4,10},{6,12},{8,14},{10,16},{12,18},{14,20},{16,22},{... | collective-permute-start | bytes 44 | tf_op jit(solution)/shard_map/ppermute | solution.py:35
  44.8 273.2 %collective-permute-start.3 = (s32[1,3]{1,0:T(1,128)}, s32[1,3]{1,0:T(1,128)}, u32[]{:S(2)}, u32[]{:S(2)}) collective-permute-start(s32[1,3]{1,0:T(1,128)} %get-tuple-element.54), channel_id=1, source_target_pairs={{0,8},{2,10},{4,12},{6,14},{8,16},{10,18},{12,20},{14,22},{16,24},... | collective-permute-start | bytes 44 | tf_op jit(solution)/shard_map/ppermute | solution.py:35
  46.3 275.4 %collective-permute-start.4 = (s32[1,3]{1,0:T(1,128)}, s32[1,3]{1,0:T(1,128)}, u32[]{:S(2)}, u32[]{:S(2)}) collective-permute-start(s32[1,3]{1,0:T(1,128)} %get-tuple-element.53), channel_id=1, source_target_pairs={{0,10},{2,12},{4,14},{6,16},{8,18},{10,20},{12,22},{14,24},{16,26}... | collective-permute-start | bytes 44 | tf_op jit(solution)/shard_map/ppermute | solution.py:35
  56.0 11.6 %copy-start.68 = (s32[16,8]{0,1:T(8,128)S(1)}, s32[16,8]{0,1:T(8,128)}, u32[]{:S(2)}) copy-start(s32[16,8]{0,1:T(8,128)} %param.35) | copy-start | bytes 1540
  88.0 9.1 %copy-start.18 = (f32[16,8,4,128]{3,2,1,0:T(4,128)S(1)}, f32[16,8,4,128]{3,2,1,0:T(4,128)}, u32[]{:S(2)}) copy-start(f32[16,8,4,128]{3,2,1,0:T(4,128)} %convert.1) | copy-start | bytes 786436
  88.0 9.2 %copy-start.1 = (f32[16,4,128,128]{3,2,1,0:T(8,128)S(1)}, f32[16,4,128,128]{3,2,1,0:T(8,128)}, u32[]{:S(2)}) copy-start(f32[16,4,128,128]{3,2,1,0:T(8,128)} %param.38) | copy-start | bytes 12582916
  88.0 9.2 %copy-start.44 = (f32[16,4]{1,0:T(8,128)S(1)}, f32[16,4]{1,0:T(8,128)}, u32[]{:S(2)}) copy-start(f32[16,4]{1,0:T(8,128)} %copy.256) | copy-start | bytes 772
  90.1 41.3 %copy-start.52 = (pred[16]{0:T(512)(128)(4,1)}, pred[16]{0:T(512)(128)(4,1)S(1)}, u32[]{:S(2)}) copy-start(pred[16]{0:T(512)(128)(4,1)S(1)} %get-tuple-element.65) | copy-start | bytes 52
  90.1 41.3 %copy-start.54 = (pred[16]{0:T(512)(128)(4,1)}, pred[16]{0:T(512)(128)(4,1)S(1)}, u32[]{:S(2)}) copy-start(pred[16]{0:T(512)(128)(4,1)S(1)} %get-tuple-element.59) | copy-start | bytes 52
  90.1 41.3 %copy-start.56 = (pred[16]{0:T(512)(128)(4,1)}, pred[16]{0:T(512)(128)(4,1)S(1)}, u32[]{:S(2)}) copy-start(pred[16]{0:T(512)(128)(4,1)S(1)} %get-tuple-element.60) | copy-start | bytes 52
  90.1 47.1 %copy-start.60 = (pred[16]{0:T(512)(128)(4,1)}, pred[16]{0:T(512)(128)(4,1)S(1)}, u32[]{:S(2)}) copy-start(pred[16]{0:T(512)(128)(4,1)S(1)} %get-tuple-element.61) | copy-start | bytes 52
  91.7 39.7 %copy-start.9 = (f32[16,4,128]{2,1,0:T(4,128)}, f32[16,4,128]{2,1,0:T(4,128)S(1)}, u32[]{:S(2)}) copy-start(f32[16,4,128]{2,1,0:T(4,128)S(1)} %get-tuple-element.14) | copy-start | bytes 98308
  91.7 39.7 %copy-start.11 = (f32[16,4,128]{2,1,0:T(4,128)}, f32[16,4,128]{2,1,0:T(4,128)S(1)}, u32[]{:S(2)}) copy-start(f32[16,4,128]{2,1,0:T(4,128)S(1)} %get-tuple-element.15) | copy-start | bytes 98308
  91.7 45.5 %copy-start.19 = (f32[16,4,128]{2,1,0:T(4,128)}, f32[16,4,128]{2,1,0:T(4,128)S(1)}, u32[]{:S(2)}) copy-start(f32[16,4,128]{2,1,0:T(4,128)S(1)} %get-tuple-element.16) | copy-start | bytes 98308
  111.2 20.3 %copy-start.13 = (f32[16,4,128]{2,1,0:T(4,128)}, f32[16,4,128]{2,1,0:T(4,128)S(1)}, u32[]{:S(2)}) copy-start(f32[16,4,128]{2,1,0:T(4,128)S(1)} %fusion.102) | copy-start | bytes 98308
  111.2 8.0 %copy-start.32 = (f32[16,4]{1,0:T(8,128)S(1)}, f32[16,4]{1,0:T(8,128)}, u32[]{:S(2)}) copy-start(f32[16,4]{1,0:T(8,128)} %copy.264) | copy-start | bytes 772
  111.2 8.0 %copy-start.51 = (f32[16,4]{1,0:T(8,128)S(1)}, f32[16,4]{1,0:T(8,128)}, u32[]{:S(2)}) copy-start(f32[16,4]{1,0:T(8,128)} %copy.253) | copy-start | bytes 772
  119.2 12.3 %copy-start.15 = (f32[16,4,128]{2,1,0:T(4,128)}, f32[16,4,128]{2,1,0:T(4,128)S(1)}, u32[]{:S(2)}) copy-start(f32[16,4,128]{2,1,0:T(4,128)S(1)} %fusion.101) | copy-start | bytes 98308
  125.6 11.6 %copy-start.4 = (f32[16,4,128,128]{3,2,1,0:T(8,128)}, f32[16,4,128,128]{3,2,1,0:T(8,128)S(1)}, u32[]{:S(2)}) copy-start(f32[16,4,128,128]{3,2,1,0:T(8,128)S(1)} %add_select_fusion.4) | copy-start | bytes 12582916
  129.3 7.9 %copy-start.21 = (f32[16,4,128]{2,1,0:T(4,128)}, f32[16,4,128]{2,1,0:T(4,128)S(1)}, u32[]{:S(2)}) copy-start(f32[16,4,128]{2,1,0:T(4,128)S(1)} %fusion.100) | copy-start | bytes 98308
  137.3 197.3 %copy-start.70 = (s32[1,3]{1,0:T(1,128)S(1)}, s32[1,3]{1,0:T(1,128)}, u32[]{:S(2)}) copy-start(s32[1,3]{1,0:T(1,128)} %get-tuple-element.43) | copy-start | bytes 40
  247.4 79.4 %collective-permute-start.5 = (s32[1,3]{1,0:T(1,128)}, s32[1,3]{1,0:T(1,128)}, u32[]{:S(2)}, u32[]{:S(2)}) collective-permute-start(s32[1,3]{1,0:T(1,128)} %get-tuple-element.52), channel_id=1, source_target_pairs={{0,12},{2,14},{4,16},{6,18},{8,20},{10,22},{12,24},{14,26},{16,28}... | collective-permute-start | bytes 44 | tf_op jit(solution)/shard_map/ppermute | solution.py:35
  248.7 79.4 %collective-permute-start.6 = (s32[1,3]{1,0:T(1,128)}, s32[1,3]{1,0:T(1,128)}, u32[]{:S(2)}, u32[]{:S(2)}) collective-permute-start(s32[1,3]{1,0:T(1,128)} %get-tuple-element.51), channel_id=1, source_target_pairs={{0,14},{2,16},{4,18},{6,20},{8,22},{10,24},{12,26},{14,28},{16,30}... | collective-permute-start | bytes 44 | tf_op jit(solution)/shard_map/ppermute | solution.py:35
  314.6 17.2 %collective-permute-start.7 = (s32[1,3]{1,0:T(1,128)}, s32[1,3]{1,0:T(1,128)}, u32[]{:S(2)}, u32[]{:S(2)}) collective-permute-start(s32[1,3]{1,0:T(1,128)} %get-tuple-element.50), channel_id=1, source_target_pairs={{0,16},{2,18},{4,20},{6,22},{8,24},{10,26},{12,28},{14,30},{16,0},... | collective-permute-start | bytes 44 | tf_op jit(solution)/shard_map/ppermute | solution.py:35
  318.1 15.0 %collective-permute-start.8 = (s32[1,3]{1,0:T(1,128)}, s32[1,3]{1,0:T(1,128)}, u32[]{:S(2)}, u32[]{:S(2)}) collective-permute-start(s32[1,3]{1,0:T(1,128)} %get-tuple-element.49), channel_id=1, source_target_pairs={{0,18},{2,20},{4,22},{6,24},{8,26},{10,28},{12,30},{14,0},{16,2},{... | collective-permute-start | bytes 44 | tf_op jit(solution)/shard_map/ppermute | solution.py:35
  321.7 12.9 %collective-permute-start.9 = (s32[1,3]{1,0:T(1,128)}, s32[1,3]{1,0:T(1,128)}, u32[]{:S(2)}, u32[]{:S(2)}) collective-permute-start(s32[1,3]{1,0:T(1,128)} %get-tuple-element.48), channel_id=1, source_target_pairs={{0,20},{2,22},{4,24},{6,26},{8,28},{10,30},{12,0},{14,2},{16,4},{1... | collective-permute-start | bytes 44 | tf_op jit(solution)/shard_map/ppermute | solution.py:35
  326.8 10.6 %collective-permute-start.10 = (s32[1,3]{1,0:T(1,128)}, s32[1,3]{1,0:T(1,128)}, u32[]{:S(2)}, u32[]{:S(2)}) collective-permute-start(s32[1,3]{1,0:T(1,128)} %get-tuple-element.47), channel_id=1, source_target_pairs={{0,22},{2,24},{4,26},{6,28},{8,30},{10,0},{12,2},{14,4},{16,6},{18... | collective-permute-start | bytes 44 | tf_op jit(solution)/shard_map/ppermute | solution.py:35
  328.1 10.6 %collective-permute-start.11 = (s32[1,3]{1,0:T(1,128)}, s32[1,3]{1,0:T(1,128)}, u32[]{:S(2)}, u32[]{:S(2)}) collective-permute-start(s32[1,3]{1,0:T(1,128)} %get-tuple-element.46), channel_id=1, source_target_pairs={{0,24},{2,26},{4,28},{6,30},{8,0},{10,2},{12,4},{14,6},{16,8},{18,... | collective-permute-start | bytes 44 | tf_op jit(solution)/shard_map/ppermute | solution.py:35
  331.7 8.2 %collective-permute-start.12 = (s32[1,3]{1,0:T(1,128)}, s32[1,3]{1,0:T(1,128)}, u32[]{:S(2)}, u32[]{:S(2)}) collective-permute-start(s32[1,3]{1,0:T(1,128)} %get-tuple-element.45), channel_id=1, source_target_pairs={{0,26},{2,28},{4,30},{6,0},{8,2},{10,4},{12,6},{14,8},{16,10},{18,... | collective-permute-start | bytes 44 | tf_op jit(solution)/shard_map/ppermute | solution.py:35
  333.0 8.2 %collective-permute-start.13 = (s32[1,3]{1,0:T(1,128)}, s32[1,3]{1,0:T(1,128)}, u32[]{:S(2)}, u32[]{:S(2)}) collective-permute-start(s32[1,3]{1,0:T(1,128)} %get-tuple-element.44), channel_id=1, source_target_pairs={{0,28},{2,30},{4,0},{6,2},{8,4},{10,6},{12,8},{14,10},{16,12},{18,... | collective-permute-start | bytes 44 | tf_op jit(solution)/shard_map/ppermute | solution.py:35
  334.6 7.9 %collective-permute-start.14 = (s32[1,3]{1,0:T(1,128)S(1)}, s32[1,3]{1,0:T(1,128)}, u32[]{:S(2)}, u32[]{:S(2)}) collective-permute-start(s32[1,3]{1,0:T(1,128)S(1)} %copy-done.70), channel_id=1, source_target_pairs={{0,30},{2,0},{4,2},{6,4},{8,6},{10,8},{12,10},{14,12},{16,14},{18,... | collective-permute-start | bytes 44 | tf_op jit(solution)/shard_map/ppermute | solution.py:35
  357.3 8.8 %copy-start.8 = (bf16[48,32,512]{2,1,0:T(8,128)(2,1)S(1)}, bf16[48,32,512]{2,1,0:T(8,128)(2,1)}, u32[]{:S(2)}) copy-start(bf16[48,32,512]{2,1,0:T(8,128)(2,1)} %gather_fusion) | copy-start | bytes 4718596
  357.3 8.8 %copy-start.43 = (pred[48,128]{1,0:T(8,128)(4,1)S(1)}, pred[48,128]{1,0:T(8,128)(4,1)}, u32[]{:S(2)}) copy-start(pred[48,128]{1,0:T(8,128)(4,1)} %add_compare_fusion) | copy-start | bytes 18436
  406.8 44.5 %all-gather.2.cloned.1.call-start = ((), (), s32[]{:S(2)}) async-start(), calls=%async_computation.5 | async-start | bytes 1572864 | tf_op jit(solution)/shard_map/all_gather | solution.py:194
  407.6 12.7 %copy-start.27 = (f32[16,4,128]{2,1,0:T(4,128)}, f32[16,4,128]{2,1,0:T(4,128)S(1)}, u32[]{:S(2)}) copy-start(f32[16,4,128]{2,1,0:T(4,128)S(1)} %fusion.99) | copy-start | bytes 98308
  407.7 12.6 %copy-start.42 = (f32[16,4]{1,0:T(8,128)}, f32[16,4]{1,0:T(8,128)S(1)}, u32[]{:S(2)}) copy-start(f32[16,4]{1,0:T(8,128)S(1)} %copy.268) | copy-start | bytes 772
  410.0 12.4 %copy-start.38 = (f32[16,1,4,128]{3,2,1,0:T(4,128)S(1)}, f32[16,1,4,128]{3,2,1,0:T(4,128)}, u32[]{:S(2)}) copy-start(f32[16,1,4,128]{3,2,1,0:T(4,128)} %get-tuple-element.20) | copy-start | bytes 98308
  430.6 66.0 %reduce-scatter.5.cloned.1.call-start = ((), (), s32[]{:S(2)}) async-start(), calls=%async_computation.6 | async-start | bytes 1572864 | tf_op jit(solution)/shard_map/reduce_scatter | solution.py:198
  (45 other events, 209.1 us)
Sparse Core Ops, SparseCore 0:
  406.9 19.5 reduce-scatter.2
  430.7 20.5 all-gather.1
  464.4 20.3 reduce-scatter.4
